TPU v7x, 32 devices: a whole 2x2x4 slice. The times are simulated.
32 devices in a mesh: groups: 2 (over x), seq: 16 (over z, y, core).
Axes of the slice: x: 2, y: 2, z: 4, core: 2. Of those that a mesh axis runs over, the one named last changes fastest.
Arguments:
- clip_tokens: bfloat16 [32, 128, 512], P(('groups', 'seq')), parts along dimension 0, may hold values from -6 to 6
- spatial_qkv: bfloat16 [512, 1536], replicated, may hold values from -4.6403883 to 4.6403883
- spatial_out: bfloat16 [512, 512], replicated, may hold values from -0.5 to 0.5
- temporal_qkv: bfloat16 [512, 1536], replicated, may hold values from -4.6403883 to 4.6403883
- temporal_out: bfloat16 [512, 512], replicated, may hold values from -0.5 to 0.5
- mlp_up: bfloat16 [512, 2048], replicated, may hold values from -0.25 to 0.25
- mlp_down: bfloat16 [2048, 512], replicated, may hold values from -0.25 to 0.25
Outputs:
- layer_out: bfloat16 [32, 128, 512], P(('groups', 'seq')), parts along dimension 0
There are 2 independent parts, one for each index of `groups`. A program takes and returns all parts, laid end to end along the dimension named above; an argument that names none is the same for every part. Nothing has to cross between parts.
All inputs are finite; a program needn't handle non-finite values.
Results may differ from a plain program's by a relative error of at most 0.013.
Values may be sent and summed in bfloat16 or wider, within the bound.
A program may use at most 128 MiB of HBM per device.

v0:
```python
import jax
import jax.numpy as jnp
from jax import lax
from jax.sharding import PartitionSpec as P

HEADS = 8


def norm_rows(values):
    center = values - jnp.mean(values, axis=-1, keepdims=True)
    spread = jnp.mean(center * center, axis=-1, keepdims=True)
    return (center * lax.rsqrt(spread + 1e-05)).astype(jnp.bfloat16)


def softmax_rows(scores):
    row_max = jnp.max(scores, axis=-1, keepdims=True)
    raised = jnp.exp(scores - row_max)
    return (raised / jnp.sum(raised, axis=-1, keepdims=True)).astype(jnp.bfloat16)


def spatial_frame(frame_rows, w_qkv, w_out):
    patches, model_width = frame_rows.shape
    head_width = model_width // HEADS
    packed = jnp.dot(
        norm_rows(frame_rows.astype(jnp.float32)), w_qkv, preferred_element_type=jnp.float32
    )
    packed = packed.astype(jnp.bfloat16).reshape(patches, 3, HEADS, head_width)
    key_rows = packed[:, 1]
    value_rows = packed[:, 2]
    block_rows = min(512, patches)
    query_rows = packed[:, 0].reshape(patches // block_rows, block_rows, HEADS, head_width)

    def one_block(query_block):
        scores = jnp.einsum(
            "qhd,khd->hqk", query_block, key_rows, preferred_element_type=jnp.float32
        ) * head_width ** (-0.5)
        weights = softmax_rows(scores)
        attended = jnp.einsum(
            "hqk,khd->qhd", weights, value_rows, preferred_element_type=jnp.float32
        )
        return attended.astype(jnp.bfloat16).reshape(block_rows, model_width)

    attended = lax.map(one_block, query_rows).reshape(patches, model_width)
    merged = frame_rows.astype(jnp.float32) + jnp.dot(
        attended, w_out, preferred_element_type=jnp.float32
    )
    return merged.astype(jnp.bfloat16)


def temporal_block(tokens, w_qkv, w_out):
    frames, count_rows, model_width = tokens.shape
    head_width = model_width // HEADS
    flat_rows = tokens.reshape(frames * count_rows, model_width)
    packed = jnp.dot(
        norm_rows(flat_rows.astype(jnp.float32)), w_qkv, preferred_element_type=jnp.float32
    )
    packed = packed.astype(jnp.bfloat16).reshape(frames, count_rows, 3, HEADS, head_width)
    scores = jnp.einsum(
        "fkhd,gkhd->khfg", packed[:, :, 0], packed[:, :, 1], preferred_element_type=jnp.float32
    ) * head_width ** (-0.5)
    weights = softmax_rows(scores)
    attended = jnp.einsum(
        "khfg,gkhd->fkhd", weights, packed[:, :, 2], preferred_element_type=jnp.float32
    )
    attended = attended.astype(jnp.bfloat16).reshape(frames * count_rows, model_width)
    merged = flat_rows.astype(jnp.float32) + jnp.dot(
        attended, w_out, preferred_element_type=jnp.float32
    )
    return merged.astype(jnp.bfloat16)


def feed_forward(tokens, w_up, w_down):
    raised = jnp.dot(
        norm_rows(tokens.astype(jnp.float32)), w_up, preferred_element_type=jnp.float32
    )
    hidden = jax.nn.gelu(raised, approximate=True).astype(jnp.bfloat16)
    merged = tokens.astype(jnp.float32) + jnp.dot(
        hidden, w_down, preferred_element_type=jnp.float32
    )
    return merged.astype(jnp.bfloat16)


def local(clip_tokens, spatial_qkv, spatial_out, temporal_qkv, temporal_out, mlp_up, mlp_down):
    frame_count, patches, model_width = clip_tokens.shape
    devices = lax.axis_size("seq")
    mixed = lax.map(
        lambda frame_rows: spatial_frame(frame_rows, spatial_qkv, spatial_out), clip_tokens
    )
    blocks = mixed.reshape(frame_count, devices, patches // devices, model_width)
    arrived = lax.all_to_all(blocks, "seq", split_axis=1, concat_axis=0, tiled=True)
    frames = arrived.shape[0]
    count_rows = arrived.shape[2]
    tokens = arrived.reshape(frames, count_rows, model_width)
    after_time = temporal_block(tokens, temporal_qkv, temporal_out)
    returned = after_time.reshape(frames, 1, count_rows, model_width)
    arrived_back = lax.all_to_all(returned, "seq", split_axis=0, concat_axis=1, tiled=True)
    result_rows = arrived_back.reshape(frame_count * patches, model_width)
    result_rows = feed_forward(result_rows, mlp_up, mlp_down)
    return result_rows.reshape(frame_count, patches, model_width)


def solution(mesh):
    in_specs = (P(("groups", "seq"), None, None), P(), P(), P(), P(), P(), P())
    out_specs = P(("groups", "seq"), None, None)
    return jax.shard_map(local, mesh=mesh, in_specs=in_specs, out_specs=out_specs, check_vma=False)
```

profile of v0, /device:TPU:0, one launch (start us, length us, event | category | flops | bytes accessed | tf_op | source)
XLA Modules:
  0.0 44.1 jit_solution(6778775718888962342)
XLA Ops:
  0.0 1.2 %convert_reduce_fusion.2 = f32[128]{0:T(128)S(1)} fusion(bf16[1,128,512]{2,1,0:T(8,128)(2,1)} %param.7), kind=kLoop, calls=%fused_computation.45 | loop fusion | flops 130944 | bytes 131584 | tf_op jit(solution)/shard_map/while/body/eval_jaxpr/reduce_sum | solution.py:10
  1.2 1.1 %fusion.31 = f32[128]{0:T(128)S(1)} fusion(bf16[1,128,512]{2,1,0:T(8,128)(2,1)} %param.7, f32[128]{0:T(128)S(1)} %broadcast_multiply_fusion.2), kind=kLoop, calls=%fused_computation.50 | loop fusion | flops 262016 | bytes 132096 | tf_op jit(solution)/shard_map/while/body/eval_jaxpr/reduce_sum | solution.py:11
  2.3 1.9 %convolution_convert_fusion.1 = bf16[128,1536]{1,0:T(8,128)(2,1)S(1)} fusion(bf16[512,1536]{1,0:T(8,128)(2,1)} %param.8, bf16[1,128,512]{2,1,0:T(8,128)(2,1)} %param.7, f32[128]{0:T(128)S(1)} %add_rsqrt_fusion.2, f32[128]{0:T(128)S(1)} %broadcast_multiply_fusion.2), kind=kOutput, calls=%fused_computation.3 | convolution fusion | flops 201785344 | bytes 2098176 | tf_op jit(solution)/shard_map/while/body/eval_jaxpr/dot_general | solution.py:24
  4.2 0.2 copy.23
  4.4 0.4 fusion.67
  4.8 1.1 %convolution_multiply_fusion = f32[8,128,128]{1,2,0:T(8,128)} fusion(bf16[128,3,8,64]{0,3,2,1:T(8,128)(2,1)S(1)} %bitcast.104), kind=kOutput, calls=%fused_computation.9 | convolution fusion | flops 16908288 | bytes 786432 | tf_op jit(solution)/shard_map/while/body/eval_jaxpr/while/body/eval_jaxpr/qhd,khd->hqk/dot_general | solution.py:34
  5.9 1.5 %convolution_convert_fusion.3 = bf16[8,64,128]{2,1,0:T(8,128)(2,1)S(1)} fusion(f32[8,128]{1,0:T(8,128)S(1)} %fusion.67, bf16[128,3,8,64]{0,3,2,1:T(8,128)(2,1)S(1)} %bitcast.105, f32[8,128,128]{1,2,0:T(8,128)} %convolution_multiply_fusion), kind=kOutput, calls=%fused_computation.19 | convolution fusion | flops 17237120 | bytes 1314816 | tf_op jit(solution)/shard_map/while/body/eval_jaxpr/while/body/eval_jaxpr/hqk,khd->qhd/dot_general | solution.py:38
  7.4 0.3 fusion.12
  7.6 15.1 %all_to_all.8 = bf16[1,16,8,512]{3,2,0,1:T(8,128)(2,1)S(1)} all-to-all(bf16[1,16,8,512]{3,2,0,1:T(8,128)(2,1)S(1)} %fusion.12), channel_id=1, replica_groups=mesh['groups'=2,'seq'=16] {'seq'}, dimensions={1} | all-to-all | bytes 262144 | tf_op jit(solution)/shard_map/all_to_all | solution.py:90
  22.8 0.1 convert_reduce_fusion.1
  23.0 0.2 fusion.38
  23.2 0.1 rsqrt.33
  23.2 1.8 %convolution_convert_fusion = bf16[128,1536]{1,0:T(8,128)(2,1)S(1)} fusion(bf16[512,1536]{1,0:T(8,128)(2,1)} %param.10, bf16[1,16,8,512]{3,2,0,1:T(8,128)(2,1)S(1)} %all_to_all.8, f32[128]{0:T(128)S(1)} %rsqrt.33, f32[128]{0:T(128)S(1)} %div.53), kind=kOutput, calls=%fused_computation.2 | convolution fusion | flops 201785344 | bytes 2098176 | tf_op jit(solution)/shard_map/dot_general | solution.py:54
  25.1 0.4 %reshape.151 = bf16[16,8,3,8,64]{4,3,2,1,0:T(8,128)(2,1)S(1)} reshape(bf16[128,1536]{1,0:T(8,128)(2,1)S(1)} %convolution_convert_fusion) | data formatting | bytes 786432 | tf_op jit(solution)/shard_map/reshape | solution.py:57
  25.5 0.9 %fusion.66 = (bf16[16,8,1,8,64]{4,3,2,1,0:T(8,128)(2,1)S(1)}, bf16[16,8,1,8,64]{4,3,2,1,0:T(8,128)(2,1)}, bf16[16,8,1,8,64]{4,3,2,1,0:T(8,128)(2,1)S(1)}) fusion(bf16[16,8,3,8,64]{4,3,2,1,0:T(8,128)(2,1)S(1)} %reshape.151), kind=kLoop, calls=%fused_computation.88 | loop fusion | bytes 786432 | tf_op jit(solution)/shard_map/slice | solution.py:59
  26.5 1.1 %fusion.68 = f32[8,8,16]{2,1,0:T(8,128)} fusion(bf16[16,8,1,8,64]{4,3,2,1,0:T(8,128)(2,1)S(1)} %get-tuple-element.40, bf16[16,8,1,8,64]{4,3,2,1,0:T(8,128)(2,1)S(1)} %get-tuple-element.33), kind=kOutput, calls=%fused_computation.90 | convolution fusion | flops 2146319 | bytes 266240 | tf_op jit(solution)/shard_map/sub | solution.py:17
  27.6 0.4 convolution_multiply_fusion.1
  28.0 1.4 %fusion.6 = bf16[16,8,8,64]{3,0,2,1:T(8,128)(2,1)S(1)} fusion(bf16[16,8,1,8,64]{4,3,2,1,0:T(8,128)(2,1)} %get-tuple-element.34, f32[8,8,16]{2,1,0:T(8,128)} %fusion.68, f32[8,8,16,16]{2,3,1,0:T(8,128)S(1)} %convolution_multiply_fusion.1), kind=kOutput, calls=%fused_computation.12 | convolution fusion | flops 2212879 | bytes 331776 | tf_op jit(solution)/shard_map/khfg,gkhd->fkhd/dot_general | solution.py:62
  29.5 0.2 reshape.152
  29.7 0.2 fusion.11
  30.0 10.5 %all_to_all.9 = bf16[16,1,8,512]{3,2,1,0:T(8,128)(2,1)S(1)} all-to-all(bf16[16,1,8,512]{3,2,1,0:T(8,128)(2,1)S(1)} %fusion.11), channel_id=1, replica_groups=mesh['groups'=2,'seq'=16] {'seq'}, dimensions={0} | all-to-all | bytes 262144 | tf_op jit(solution)/shard_map/all_to_all | solution.py:96
  40.5 0.1 convert_reduce_fusion
  40.7 0.2 fusion.40
  41.0 3.2 %fusion.10 = bf16[1,128,512]{2,1,0:T(8,128)(2,1)} fusion(bf16[2048,512]{1,0:T(8,128)(2,1)S(1)} %copy-done, bf16[16,1,8,512]{3,2,1,0:T(8,128)(2,1)S(1)} %all_to_all.9, bf16[512,2048]{1,0:T(8,128)(2,1)} %param.12, f32[128]{0:T(128)S(1)} %rsqrt.35, f32[128]{0:T(128)S(1)} %div.58), kind=kOutput, calls=%fused_computation.20 | convolution fusion | flops 539688960 | bytes 4457472 | tf_op jit(solution)/shard_map/dot_general | solution.py:77
  (18 shorter events, 0.4 us)
Async XLA Ops:
  0.0 41.0 %copy-start = (bf16[2048,512]{1,0:T(8,128)(2,1)S(1)}, bf16[2048,512]{1,0:T(8,128)(2,1)}, u32[]{:S(2)}) copy-start(bf16[2048,512]{1,0:T(8,128)(2,1)} %param.13) | copy-start | bytes 6291460
  4.4 3.0 %copy-start.1 = (bf16[1,128,512]{2,1,0:T(8,128)(2,1)S(1)}, bf16[1,128,512]{2,1,0:T(8,128)(2,1)}, u32[]{:S(2)}) copy-start(bf16[1,128,512]{2,1,0:T(8,128)(2,1)} %param.7) | copy-start | bytes 393220
  4.4 3.0 %copy-start.2 = (bf16[512,512]{1,0:T(8,128)(2,1)S(1)}, bf16[512,512]{1,0:T(8,128)(2,1)}, u32[]{:S(2)}) copy-start(bf16[512,512]{1,0:T(8,128)(2,1)} %param.9) | copy-start | bytes 1572868
  28.0 1.7 %copy-start.3 = (bf16[512,512]{1,0:T(8,128)(2,1)S(1)}, bf16[512,512]{1,0:T(8,128)(2,1)}, u32[]{:S(2)}) copy-start(bf16[512,512]{1,0:T(8,128)(2,1)} %param.11) | copy-start | bytes 1572868
where the time goes:
time: 44.5 us; the launch traced here: 44.1 us
  blocking collectives  25.6 us (58%)
  matrix products  13.3 us (30%)
  other arithmetic  2.81 us (6%)
  local copies, waits for them, and re-layouts  2.23 us (5%)
    all_to_all x1, blocking collectives, local(): lax.all_to_all(blocks, 'seq', split_axis=1, concat_axis=0, tiled=True)  15.1 us
    all_to_all x1, blocking collectives, local(): lax.all_to_all(returned, 'seq', split_axis=0, concat_axis=1, tiled=True)  10.5 us
    dot_general x1, matrix products, feed_forward(): jnp.dot(hidden, w_down, preferred_element_type=jnp.float32)  3.19 us
    dot_general x1, matrix products, spatial_frame(): jnp.dot(norm_rows(frame_rows.astype(jnp.float32)), w_qkv, preferred_eleme...  1.9 us
    dot_general x1, matrix products, temporal_block(): jnp.dot(norm_rows(flat_rows.astype(jnp.float32)), w_qkv, preferred_elemen...  1.82 us
    sub x2, matrix products, softmax_rows(): raised = jnp.exp(scores - row_max)  1.51 us
    dot_general x1, matrix products, one_block(): jnp.einsum('hqk,khd->qhd', weights, value_rows, preferred_element_type=jn...  1.47 us
    reduce_sum x3, other arithmetic, norm_rows(): spread = jnp.mean(center * center, axis=-1, keepdims=True)  1.43 us

commit v1 on v0

v1 whole, which is shorter than its diff:
```python
import functools
import math

import jax
import jax.numpy as jnp
from jax import lax
from jax.experimental import pallas as pl
from jax.experimental.pallas import tpu as pltpu
from jax.sharding import PartitionSpec as P

HEADS = 8
LANES = 128
MESH = pl.DeviceIdType.MESH
F32 = jnp.float32
BF16 = jnp.bfloat16


def norm_rows(values):
    center = values - jnp.mean(values, axis=-1, keepdims=True)
    spread = jnp.mean(center * center, axis=-1, keepdims=True)
    return (center * lax.rsqrt(spread + 1e-05)).astype(BF16)


def gelu(u):
    return 0.5 * u * (1.0 + jnp.tanh(math.sqrt(2.0 / math.pi) * (u + 0.044715 * (u * u * u))))


def dot(a, b):
    return jnp.dot(a, b, preferred_element_type=F32)


def blocks_of(count, body):
    if count <= 2:
        for i in range(count):
            body(i)
    else:
        def step(i, carry):
            body(i)
            return carry

        lax.fori_loop(0, count, step, 0)


def attend(packed, first_row, rows, width, head_width, same_slot):
    total = packed.shape[0]
    per_block = LANES // head_width
    lane = lax.broadcasted_iota(jnp.int32, (rows, LANES), 1)
    ones = jnp.ones((total, LANES), BF16)
    scale = head_width ** (-0.5) * math.log2(math.e)
    if same_slot:
        query_at = lax.broadcasted_iota(jnp.int32, (per_block * rows, total), 0)
        key_at = lax.broadcasted_iota(jnp.int32, (per_block * rows, total), 1)
        allowed = lax.rem(query_at, same_slot) == lax.rem(key_at, same_slot)
    outs = []
    for block in range(width // LANES):
        q = packed[pl.ds(first_row, rows), pl.ds(block * LANES, LANES)]
        k = packed[:, pl.ds(width + block * LANES, LANES)]
        v = packed[:, pl.ds(2 * width + block * LANES, LANES)]
        split = [
            jnp.where((lane >= h * head_width) & (lane < (h + 1) * head_width), q, jnp.zeros_like(q))
            for h in range(per_block)
        ]
        scores = lax.dot_general(
            jnp.concatenate(split, axis=0), k, (((1,), (1,)), ((), ())), preferred_element_type=F32
        )
        if same_slot:
            scores = jnp.where(allowed, scores, -1e30)
        top = jnp.max(scores, axis=-1, keepdims=True)
        raised = jnp.exp2((scores - top) * scale).astype(BF16)
        both = dot(raised, jnp.concatenate([v, ones], axis=1))
        mixed = both[:, :LANES] / both[:, LANES:]
        out = mixed[:rows]
        for h in range(1, per_block):
            out = jnp.where(lane >= h * head_width, mixed[h * rows:(h + 1) * rows], out)
        outs.append(out.astype(BF16))
    return jnp.concatenate(outs, axis=1)


def kernel(
    n, x_hbm, wq1_hbm, wo1_hbm, wq2_hbm, wo2_hbm, up_hbm, down_hbm, out_hbm,
    x_v, wq1, wo1, wq2, wo2, up, down, packed, send1, recv1, send2,
    load_sem, send1_sem, recv1_sem, send2_sem, recv2_sem,
):
    _, slot, width = x_v.shape
    total = n * slot
    head_width = width // HEADS
    half = n // 2
    me = lax.axis_index("seq")
    side = me // half
    near, far = side * half, (1 - side) * half
    place = lax.rem(me, half)

    def load(i, src, dst):
        return pltpu.make_async_copy(src, dst, load_sem.at[i])

    loads = [
        load(i, src, dst) for i, (src, dst) in enumerate(
            ((x_hbm, x_v), (wq1_hbm, wq1), (wo1_hbm, wo1), (wq2_hbm, wq2), (wo2_hbm, wo2), (up_hbm, up), (down_hbm, down))
        )
    ]
    loads[0].start()
    loads[1].start()

    def far_peer(j):
        return far + lax.rem(place + j, half)

    def near_peer(j):
        return near + lax.rem(place + j, half)

    def each(first, body):
        def step(j, carry):
            body(j)
            return carry

        lax.fori_loop(first, half, step, 0, unroll=half <= 8)

    barrier = pltpu.get_barrier_semaphore()
    each(0, lambda j: pl.semaphore_signal(barrier, inc=1, device_id={"seq": far_peer(j)}, device_id_type=MESH))
    each(1, lambda j: pl.semaphore_signal(barrier, inc=1, device_id={"seq": near_peer(j)}, device_id_type=MESH))

    def copy1(peer, source):
        return pltpu.make_async_remote_copy(
            src_ref=send1.at[peer], dst_ref=recv1.at[source], send_sem=send1_sem.at[peer],
            recv_sem=recv1_sem.at[source], device_id={"seq": peer}, device_id_type=MESH,
        )

    def copy2(peer, source):
        return pltpu.make_async_remote_copy(
            src_ref=send2.at[peer], dst_ref=out_hbm.at[source], send_sem=send2_sem.at[peer],
            recv_sem=recv2_sem.at[source], device_id={"seq": peer}, device_id_type=MESH,
        )

    def every_peer(body):
        each(0, lambda j: body(far_peer(j)))
        each(1, lambda j: body(near_peer(j)))

    row_block = min(128, total)
    slots_block = row_block // slot

    def project(source, weights, i):
        rows = source[pl.ds(i * slots_block, slots_block)].astype(F32).reshape(row_block, width)
        packed[pl.ds(i * row_block, row_block), :] = dot(norm_rows(rows), weights[...]).astype(BF16)

    part = min(64, half * slot)
    part_slots = part // slot
    parts = half // part_slots

    loads[0].wait()
    loads[1].wait()
    for i in range(2, 7):
        loads[i].start()
    blocks_of(total // row_block, functools.partial(project, x_v, wq1))

    def spatial(base, i):
        first = base + i * part_slots
        heads = attend(packed, pl.multiple_of(first * slot, part), part, width, head_width, 0)
        rows = x_v[pl.ds(first, part_slots)].astype(F32).reshape(part, width)
        merged = rows + dot(heads, wo1[...])
        send1[pl.ds(first, part_slots)] = merged.reshape(part_slots, slot, width).astype(BF16)

    loads[2].wait()
    blocks_of(parts, functools.partial(spatial, far))
    pl.semaphore_wait(barrier, n - 1)
    each(0, lambda j: copy1(far_peer(j), me).start())
    blocks_of(parts, functools.partial(spatial, near))
    each(1, lambda j: copy1(near_peer(j), me).start())
    recv1[me] = send1[me]

    for i in range(3, 7):
        loads[i].wait()
    every_peer(lambda peer: copy1(me, peer).wait_recv())
    blocks_of(total // row_block, functools.partial(project, recv1, wq2))

    def temporal(base, i):
        first = base + i * part_slots
        heads = attend(packed, pl.multiple_of(first * slot, part), part, width, head_width, slot)
        rows = recv1[pl.ds(first, part_slots)].astype(F32).reshape(part, width)
        after = (rows + dot(heads, wo2[...])).astype(BF16).astype(F32)
        hidden = gelu(dot(norm_rows(after), up[...])).astype(BF16)
        done = after + dot(hidden, down[...])
        send2[pl.ds(first, part_slots)] = done.reshape(part_slots, slot, width).astype(BF16)

    blocks_of(parts, functools.partial(temporal, far))
    each(0, lambda j: copy2(far_peer(j), me).start())
    blocks_of(parts, functools.partial(temporal, near))
    each(1, lambda j: copy2(near_peer(j), me).start())
    own = pltpu.make_async_copy(send2.at[me], out_hbm.at[me], load_sem.at[0])
    own.start()
    every_peer(lambda peer: copy1(peer, me).wait_send())
    own.wait()
    every_peer(lambda peer: copy2(peer, me).wait_send())
    every_peer(lambda peer: copy2(me, peer).wait_recv())


def solution(mesh):
    n = mesh.shape["seq"]

    def local(clip_tokens, *weights):
        frames, patches, width = clip_tokens.shape
        assert frames == 1
        slot = patches // n
        blocks = (n, slot, width)
        vmem = [pltpu.VMEM(w.shape, w.dtype) for w in weights]
        out = pl.pallas_call(
            functools.partial(kernel, n),
            out_shape=jax.ShapeDtypeStruct(blocks, BF16),
            in_specs=[pl.BlockSpec(memory_space=pl.ANY)] * 7,
            out_specs=pl.BlockSpec(memory_space=pl.ANY),
            scratch_shapes=[
                pltpu.VMEM(blocks, BF16),
                *vmem,
                pltpu.VMEM((patches, 3 * width), BF16),
                pltpu.VMEM(blocks, BF16),
                pltpu.VMEM(blocks, BF16),
                pltpu.VMEM(blocks, BF16),
                pltpu.SemaphoreType.DMA((7,)),
                pltpu.SemaphoreType.DMA((n,)),
                pltpu.SemaphoreType.DMA((n,)),
                pltpu.SemaphoreType.DMA((n,)),
                pltpu.SemaphoreType.DMA((n,)),
            ],
            compiler_params=pltpu.CompilerParams(collective_id=0, has_side_effects=True),
            name="layer",
        )(clip_tokens.reshape(blocks), *weights)
        return out.reshape(frames, patches, width)

    in_specs = (P(("groups", "seq"), None, None), P(), P(), P(), P(), P(), P())
    out_specs = P(("groups", "seq"), None, None)
    return jax.shard_map(local, mesh=mesh, in_specs=in_specs, out_specs=out_specs, check_vma=False)
```

time: 44.5 us -> 21.1 us (0.47)
  blocking collectives: 25.6 us -> 0 us
  Pallas kernels: 0 us -> 19.4 us
  matrix products: 13.3 us -> 0 us
  other arithmetic: 2.81 us -> 0 us
  local copies, waits for them, and re-layouts: 2.23 us -> 1.57 us
    all_to_all x2 -> x0, blocking collectives: 25.6 us -> none  [the longest x1 15.1 us: local(): lax.all_to_all(blocks, 'seq', split_axis=1, concat_axis=0, tiled=True)]
    pallas_call x0 -> x1, Pallas kernels: none -> 19.4 us  [local(): pl.pallas_call(functools.partial(kernel, n), out_shape=jax.ShapeDtypeStru...]
    dot_general x9 -> x0, matrix products: 11.8 us -> none  [the longest x1 3.19 us: feed_forward(): jnp.dot(hidden, w_down, preferred_element_type=jnp.float32)]
    reduce_sum x6 -> x0, other arithmetic: 2.78 us -> none  [the longest x3 1.43 us: norm_rows(): spread = jnp.mean(center * center, axis=-1, keepdims=True)]
    unnamed x8 -> x1, local copies, waits for them, and re-layouts: 0.02 us -> 1.57 us
    sub x2 -> x0, matrix products: 1.51 us -> none  [softmax_rows(): raised = jnp.exp(scores - row_max)]
    slice x1 -> x0, local copies, waits for them, and re-layouts: 0.93 us -> none  [temporal_block(): packed[:, :, 0]]
    reshape x2 -> x0, local copies, waits for them, and re-layouts: 0.66 us -> none  [the longest x1 0.45 us: temporal_block(): packed.astype(jnp.bfloat16)]
where the time goes in v1:
time: 21.1 us; the launch traced here: 21 us
  Pallas kernels  19.4 us (92%)
  local copies, waits for them, and re-layouts  1.57 us (7%)
    pallas_call x1, Pallas kernels, local(): pl.pallas_call(functools.partial(kernel, n), out_shape=jax.ShapeDtypeStru...  19.4 us
    unnamed x1, local copies, waits for them, and re-layouts  1.57 us

profile of v1, /device:TPU:0, one launch (start us, length us, event | category | flops | bytes accessed | tf_op | source)
XLA Modules:
  0.0 21.0 jit_solution(11780855852488151339)
XLA Ops:
  0.0 19.4 %layer.1 = bf16[16,8,512]{2,1,0:T(8,128)(2,1)} custom-call(bf16[16,8,512]{2,1,0:T(8,128)(2,1)} %bitcast.3, bf16[512,1536]{1,0:T(8,128)(2,1)} %wq1_hbm.1, bf16[512,512]{1,0:T(8,128)(2,1)} %wo1_hbm.1, bf16[512,1536]{1,0:T(8,128)(2,1)} %wq2_hbm.1, bf16[512,512]{1,0:T(8,128)(2,1)} %wo2_hbm.1, bf16[512,2048]{1,0:T(8,128)(2,1)} %up_hbm.1, bf16[2048,512]{1,0:T(8,128)(2,1)} %down_hbm.1), custom_call_target="tpu_custom_call" | custom-call | tf_op jit(solution)/shard_map/layer/pallas_call | solution.py:204
  19.4 1.6 %copy.9 = bf16[1,128,512]{2,1,0:T(8,128)(2,1)} copy(bf16[1,128,512]{2,1,0:T(8,128)(2,1)} %bitcast.2) | data formatting | bytes 262144

commit v2 on v1

--- a/solution.py
+++ b/solution.py
@@ -10,6 +10,7 @@
 
 HEADS = 8
 LANES = 128
+VMEM_BYTES = 67043328
 MESH = pl.DeviceIdType.MESH
 F32 = jnp.float32
 BF16 = jnp.bfloat16
@@ -77,7 +78,7 @@
 
 
 def kernel(
-    n, x_hbm, wq1_hbm, wo1_hbm, wq2_hbm, wo2_hbm, up_hbm, down_hbm, out_hbm,
+    n, x_hbm, wq1_hbm, wo1_hbm, wq2_hbm, wo2_hbm, up_hbm, down_hbm, out_v,
     x_v, wq1, wo1, wq2, wo2, up, down, packed, send1, recv1, send2,
     load_sem, send1_sem, recv1_sem, send2_sem, recv2_sem,
 ):
@@ -126,7 +127,7 @@
 
     def copy2(peer, source):
         return pltpu.make_async_remote_copy(
-            src_ref=send2.at[peer], dst_ref=out_hbm.at[source], send_sem=send2_sem.at[peer],
+            src_ref=send2.at[peer], dst_ref=out_v.at[source], send_sem=send2_sem.at[peer],
             recv_sem=recv2_sem.at[source], device_id={"seq": peer}, device_id_type=MESH,
         )
 
@@ -184,12 +185,16 @@
     each(0, lambda j: copy2(far_peer(j), me).start())
     blocks_of(parts, functools.partial(temporal, near))
     each(1, lambda j: copy2(near_peer(j), me).start())
-    own = pltpu.make_async_copy(send2.at[me], out_hbm.at[me], load_sem.at[0])
-    own.start()
+    out_v[me] = send2[me]
     every_peer(lambda peer: copy1(peer, me).wait_send())
-    own.wait()
     every_peer(lambda peer: copy2(peer, me).wait_send())
     every_peer(lambda peer: copy2(me, peer).wait_recv())
+
+
+def store(rows_v, out_hbm, sem):
+    copy = pltpu.make_async_copy(rows_v, out_hbm, sem)
+    copy.start()
+    copy.wait()
 
 
 def solution(mesh):
@@ -203,9 +208,9 @@
         vmem = [pltpu.VMEM(w.shape, w.dtype) for w in weights]
         out = pl.pallas_call(
             functools.partial(kernel, n),
-            out_shape=jax.ShapeDtypeStruct(blocks, BF16),
-            in_specs=[pl.BlockSpec(memory_space=pl.ANY)] * 7,
-            out_specs=pl.BlockSpec(memory_space=pl.ANY),
+            out_shape=pltpu.VMEM(blocks, BF16),
+            in_specs=[pl.BlockSpec(memory_space=pltpu.HBM)] * 7,
+            out_specs=pl.BlockSpec(memory_space=pltpu.VMEM),
             scratch_shapes=[
                 pltpu.VMEM(blocks, BF16),
                 *vmem,
@@ -219,7 +224,7 @@
                 pltpu.SemaphoreType.DMA((n,)),
                 pltpu.SemaphoreType.DMA((n,)),
             ],
-            compiler_params=pltpu.CompilerParams(collective_id=0, has_side_effects=True),
+            compiler_params=pltpu.CompilerParams(collective_id=0, has_side_effects=True, vmem_limit_bytes=VMEM_BYTES - math.prod(blocks) * 2 - 65536),
             name="layer",
         )(clip_tokens.reshape(blocks), *weights)
         return out.reshape(frames, patches, width)

time: 21.1 us -> 20.1 us (0.953)
  local copies, waits for them, and re-layouts: 1.57 us -> 0.66 us
    unnamed x1, local copies, waits for them, and re-layouts: 1.57 us -> 0.66 us
where the time goes in v2:
time: 20.1 us; the launch traced here: 19.9 us
  Pallas kernels  19.3 us (96%)
  local copies, waits for them, and re-layouts  0.66 us (3%)
    pallas_call x1, Pallas kernels, local(): pl.pallas_call(functools.partial(kernel, n), out_shape=pltpu.VMEM(blocks,...  19.3 us
    unnamed x1, local copies, waits for them, and re-layouts  0.66 us

profile of v2, /device:TPU:0, one launch (start us, length us, event | category | flops | bytes accessed | tf_op | source)
XLA Modules:
  0.0 19.9 jit_solution(8242733775729883072)
XLA Ops:
  0.0 19.3 %layer.1 = bf16[16,8,512]{2,1,0:T(8,128)(2,1)S(1)} custom-call(bf16[16,8,512]{2,1,0:T(8,128)(2,1)} %bitcast.3, bf16[512,1536]{1,0:T(8,128)(2,1)} %wq1_hbm.1, bf16[512,512]{1,0:T(8,128)(2,1)} %wo1_hbm.1, bf16[512,1536]{1,0:T(8,128)(2,1)} %wq2_hbm.1, bf16[512,512]{1,0:T(8,128)(2,1)} %wo2_hbm.1, bf16[512,2048]{1,0:T(8,128)(2,1)} %up_hbm.1, ...), custom_call_target="tpu_custom_call" | custom-call | tf_op jit(solution)/shard_map/layer/pallas_call | solution.py:209
  19.3 0.7 %copy.9 = bf16[1,128,512]{2,1,0:T(8,128)(2,1)} copy(bf16[1,128,512]{2,1,0:T(8,128)(2,1)S(1)} %bitcast.2) | data formatting | bytes 262144

commit v3 on v2

--- a/solution.py
+++ b/solution.py
@@ -79,7 +79,7 @@
 
 def kernel(
     n, x_hbm, wq1_hbm, wo1_hbm, wq2_hbm, wo2_hbm, up_hbm, down_hbm, out_v,
-    x_v, wq1, wo1, wq2, wo2, up, down, packed, send1, recv1, send2,
+    x_v, wq1, wo1, wq2, wo2, up, down, packed, normed, send1, recv1, send2,
     load_sem, send1_sem, recv1_sem, send2_sem, recv2_sem,
 ):
     _, slot, width = x_v.shape
@@ -99,8 +99,11 @@
             ((x_hbm, x_v), (wq1_hbm, wq1), (wo1_hbm, wo1), (wq2_hbm, wq2), (wo2_hbm, wo2), (up_hbm, up), (down_hbm, down))
         )
     ]
+    bands = [pl.ds(b * width, width) for b in range(3)]
+    band_loads = [load(i, wq1_hbm.at[:, band], wq1.at[:, band]) for i, band in zip((1, 7, 8), bands)]
     loads[0].start()
-    loads[1].start()
+    for band_load in band_loads:
+        band_load.start()
 
     def far_peer(j):
         return far + lax.rem(place + j, half)
@@ -147,10 +150,21 @@
     parts = half // part_slots
 
     loads[0].wait()
-    loads[1].wait()
     for i in range(2, 7):
         loads[i].start()
-    blocks_of(total // row_block, functools.partial(project, x_v, wq1))
+
+    def normalise(i):
+        rows = x_v[pl.ds(i * slots_block, slots_block)].astype(F32).reshape(row_block, width)
+        normed[pl.ds(i * row_block, row_block), :] = norm_rows(rows)
+
+    def project_band(band, i):
+        at = pl.ds(i * row_block, row_block)
+        packed[at, band] = dot(normed[at, :], wq1[:, band]).astype(BF16)
+
+    blocks_of(total // row_block, normalise)
+    for band, band_load in zip(bands, band_loads):
+        band_load.wait()
+        blocks_of(total // row_block, functools.partial(project_band, band))
 
     def spatial(base, i):
         first = base + i * part_slots
@@ -215,10 +229,11 @@
                 pltpu.VMEM(blocks, BF16),
                 *vmem,
                 pltpu.VMEM((patches, 3 * width), BF16),
-                pltpu.VMEM(blocks, BF16),
-                pltpu.VMEM(blocks, BF16),
-                pltpu.VMEM(blocks, BF16),
-                pltpu.SemaphoreType.DMA((7,)),
+                pltpu.VMEM((patches, width), BF16),
+                pltpu.VMEM(blocks, BF16),
+                pltpu.VMEM(blocks, BF16),
+                pltpu.VMEM(blocks, BF16),
+                pltpu.SemaphoreType.DMA((9,)),
                 pltpu.SemaphoreType.DMA((n,)),
                 pltpu.SemaphoreType.DMA((n,)),
                 pltpu.SemaphoreType.DMA((n,)),

time: 20.1 us -> 20 us (level)
  no operation moved by 1% of the time
where the time goes in v3:
time: 20 us; the launch traced here: 19.8 us
  Pallas kernels  19.2 us (96%)
  local copies, waits for them, and re-layouts  0.66 us (3%)
    pallas_call x1, Pallas kernels, local(): pl.pallas_call(functools.partial(kernel, n), out_shape=pltpu.VMEM(blocks,...  19.2 us
    unnamed x1, local copies, waits for them, and re-layouts  0.66 us

profile of v3, /device:TPU:0, one launch (start us, length us, event | category | flops | bytes accessed | tf_op | source)
XLA Modules:
  0.0 19.8 jit_solution(1521808431663847971)
XLA Ops:
  0.0 19.2 %layer.1 = bf16[16,8,512]{2,1,0:T(8,128)(2,1)S(1)} custom-call(bf16[16,8,512]{2,1,0:T(8,128)(2,1)} %bitcast.3, bf16[512,1536]{1,0:T(8,128)(2,1)} %wq1_hbm.1, bf16[512,512]{1,0:T(8,128)(2,1)} %wo1_hbm.1, bf16[512,1536]{1,0:T(8,128)(2,1)} %wq2_hbm.1, bf16[512,512]{1,0:T(8,128)(2,1)} %wo2_hbm.1, bf16[512,2048]{1,0:T(8,128)(2,1)} %up_hbm.1, ...), custom_call_target="tpu_custom_call" | custom-call | tf_op jit(solution)/shard_map/layer/pallas_call | solution.py:223
  19.2 0.7 %copy.9 = bf16[1,128,512]{2,1,0:T(8,128)(2,1)} copy(bf16[1,128,512]{2,1,0:T(8,128)(2,1)S(1)} %bitcast.2) | data formatting | bytes 262144
